TPU v7x, 32 devices: a whole 2x2x4 slice. The times are simulated.
32 devices in a mesh: row: 8 (over z, x), col: 4 (over y, core).
Axes of the slice: x: 2, y: 2, z: 4, core: 2. Of those that a mesh axis runs over, the one named last changes fastest.
Arguments:
- src_points: bfloat16 [64, 8192], P(None, ('row', 'col')), may hold values from -24 to 24
- tgt_points: bfloat16 [64, 4096], P(None, ('col', 'row')), may hold values from -24 to 24
- grad_f: float32 [8192], P('row'), may hold values from -6 to 6
- grad_g: float32 [4096], P('col'), may hold values from -6 to 6
Outputs:
- grad_src: float32 [64, 8192], P(None, ('row', 'col'))
- grad_tgt: float32 [64, 4096], P(None, ('col', 'row'))
All inputs are finite; a program needn't handle non-finite values.
Results may differ from a plain program's by a relative error of at most 0.0085.
Values may be sent and summed in bfloat16 or wider, within the bound.
No kernel may reach another device: no remote copies, remote signals or barrier semaphores. Data moves between devices by JAX's collectives and lax.ppermute only.
A program may use at most 64 MiB of HBM per device.

v0:
```python
import functools
import math

import jax
import jax.numpy as jnp
from jax import lax
from jax.experimental import pallas as pl
from jax.experimental.pallas import tpu as pltpu
from jax.sharding import PartitionSpec as P


CG = 3
EPS = 4.0
TAU = 0.1
AXES = ("row", "col")
LOW = -3.0e38
TINY = 2.0**-80
LIMIT = 80.0
SPAN = 4096
ELEMENTS = 4 * 1024 * 1024
LOG2E = math.log2(math.e)
CROSS = 2.0 * LOG2E / EPS
SQUARE = LOG2E / EPS
F32 = jnp.float32
BF16 = jnp.bfloat16
NT = (((1,), (1,)), ((), ()))
VMEM = pl.BlockSpec(memory_space=pltpu.VMEM)
SMEM = pl.BlockSpec(memory_space=pltpu.SMEM)


def split3(vector):
    high = vector.astype(BF16).astype(F32)
    rest = vector - high
    mid = rest.astype(BF16).astype(F32)
    low = rest - mid
    shape = (8, vector.shape[1])
    line = lax.broadcasted_iota(jnp.int32, shape, 0)
    zero = jnp.zeros(shape, F32)
    rows = jnp.where(line == 0, high, jnp.where(line == 1, mid, jnp.where(line == 2, low, zero)))
    return rows.astype(BF16)


def total(vector):
    return jnp.sum(vector, axis=1, keepdims=True)


def fold(rows):
    return jnp.sum(rows, axis=0, keepdims=True)


def down(vector):
    return jnp.broadcast_to(vector, (128, vector.shape[1])).T


def over(wide, step, carry):
    span = min(wide, SPAN)
    if wide == span:
        return step(0, carry)
    return lax.fori_loop(0, wide // span, lambda i, c: step(pl.multiple_of(i * span, span), c), carry)


def lanes(base, offset, size):
    return pl.ds(pl.multiple_of(base + offset, 128), size) if not isinstance(base, int) else pl.ds(base + offset, size)


def pack_kernel(columns, me_ref, src_ref, tgt_ref, gf_ref, x_ref, y_ref, f_ref):
    f_ref[...] = pick(gf_ref[...], me_ref[0] % columns, src_ref.shape[1])
    x_ref[0] = src_ref[...]
    y_ref[0] = tgt_ref[...]


def lse_kernel(
    group, br, me_ref, x_ref, y_ref, lhs_ref, rhs_ref, yc_ref, p_ref, r_ref, lse_ref, sa_ref, sb_ref, acc_ref, m_ref
):
    me = me_ref[0]
    replicas, _, ns = x_ref.shape
    devices, features, nt = y_ref.shape
    rows, wide = p_ref.shape
    extra = lhs_ref.shape[1] - 3 * features
    lhs_ref[:, 3 * features :] = jnp.ones((rows, extra), BF16)
    for k in range(replicas):
        points = x_ref[k, :features, :].T
        for c in range(3):
            lhs_ref[k * ns : (k + 1) * ns, c * features : (c + 1) * features] = points
    yc_ref[features:, :] = jnp.ones((yc_ref.shape[0] - features, wide), BF16)
    for t in range(devices):
        cs = slice(t * nt, (t + 1) * nt)
        k = jnp.bitwise_xor(t, me)
        inner = k % group
        points = y_ref[(inner % 2) * (devices // 2) + (inner // 2) * replicas + k // group]
        yc_ref[:features, cs] = points
        points = points.astype(F32)
        square = fold(points * points) * -SQUARE
        value = points * CROSS
        high = value.astype(BF16)
        rest = value - high.astype(F32)
        mid = rest.astype(BF16)
        rhs_ref[:features, cs] = high
        rhs_ref[features : 2 * features, cs] = mid
        rhs_ref[2 * features : 3 * features, cs] = (rest - mid.astype(F32)).astype(BF16)
        rhs_ref[3 * features : 3 * features + 8, cs] = split3(square)
        rhs_ref[3 * features + 8 :, cs] = jnp.zeros((extra - 8, nt), BF16)
    scratch = (sa_ref, sb_ref)

    def scores(b):
        lb = lhs_ref[b * br : (b + 1) * br, :]
        s_ref = scratch[b % 2]

        def step(base, high):
            for u in range(0, min(wide, SPAN), 256):
                cs = lanes(base, u, 256)
                s = jnp.dot(lb, rhs_ref[:, cs], preferred_element_type=F32)
                s_ref[:, cs] = s
                high = jnp.maximum(high, jnp.maximum(s[:, :128], s[:, 128:]))
            return high

        return jnp.max(over(wide, step, jnp.full((br, 128), LOW, F32)), axis=1, keepdims=True)

    def exps(b, high):
        s_ref = scratch[b % 2]
        rs = slice(b * br, (b + 1) * br)
        hb = jnp.broadcast_to(high, (br, 128))

        def step(base, acc):
            for u in range(0, min(wide, SPAN), 128):
                cs = lanes(base, u, 128)
                e = jnp.exp2(s_ref[:, cs] - hb)
                p_ref[rs, cs] = e.astype(BF16)
                acc = acc + e
            return acc

        sums = jnp.sum(over(wide, step, jnp.zeros((br, 128), F32)), axis=1, keepdims=True)
        r_ref[rs, :] = jnp.broadcast_to(-(high + jnp.log2(sums)), (br, 128))
        return jnp.broadcast_to(1.0 / sums, (br, 128)).T[:1]

    count = rows // br
    inverse = []
    high = scores(0)
    for b in range(count):
        after = scores(b + 1) if b + 1 < count else None
        inverse.append(exps(b, high))
        high = after
    s = pulled(p_ref, jnp.concatenate(inverse, axis=1))
    lse_ref[...] = jnp.log2(jnp.maximum(s, TINY))

    @pl.when(jnp.min(s) < TINY)
    def _():
        acc_ref[...] = jnp.zeros(acc_ref.shape, F32)
        m_ref[...] = jnp.full(m_ref.shape, LOW, F32)

        def step(i, _):
            _, cs, v = tile_scores(i, lhs_ref, rhs_ref, r_ref)
            v = v.reshape(v.shape[0] // 8, 8, 128)
            old = m_ref[:, cs]
            new = jnp.maximum(old, jnp.max(v, axis=0))
            acc_ref[:, cs] = acc_ref[:, cs] * jnp.exp2(old - new) + fold3(jnp.exp2(v - new[None]))
            m_ref[:, cs] = new
            return 0

        lax.fori_loop(0, (rows // 128) * (wide // 128), step, 0)
        m = m_ref[...]
        top = jnp.max(m, axis=0, keepdims=True)
        lse_ref[...] = top + jnp.log2(fold(acc_ref[...] * jnp.exp2(m - top)))


def fold3(values):
    return jnp.sum(values, axis=0)


def tile_scores(i, lhs_ref, rhs_ref, r_ref):
    across = rhs_ref.shape[1] // 128
    rs = pl.ds(pl.multiple_of(i // across * 128, 128), 128)
    cs = pl.ds(pl.multiple_of(i % across * 128, 128), 128)
    return rs, cs, jnp.dot(lhs_ref[rs, :], rhs_ref[:, cs], preferred_element_type=F32) + r_ref[rs, :]


def pushed(p_ref, w):
    return fold(lax.dot_general(split3(w), p_ref[...], NT, preferred_element_type=F32))


def pulled(p_ref, y):
    return fold(jnp.dot(split3(y), p_ref[...], preferred_element_type=F32))


def plan_kernel(count, shift, *refs):
    parts, (lhs_ref, rhs_ref, r_ref, old_ref, p_ref, scale_ref, a_ref, s_ref) = refs[:count], refs[count:]
    top = functools.reduce(jnp.maximum, [q[...] for q in parts])
    c = shift - top - jnp.log2(sum(jnp.exp2(q[...] - top) for q in parts))
    rows, wide = p_ref.shape
    plain = jnp.max(c) <= LIMIT
    scale_ref[...] = jnp.exp2(jnp.minimum(c, LIMIT))

    @pl.when(jnp.logical_not(plain))
    def _():
        scale_ref[...] = c

        def step(i, _):
            rs, cs, v = tile_scores(i, lhs_ref, rhs_ref, r_ref)
            p_ref[rs, cs] = jnp.exp2(v + scale_ref[:, cs]).astype(BF16)
            return 0

        lax.fori_loop(0, (rows // 128) * (wide // 128), step, 0)
        scale_ref[...] = jnp.ones((1, wide), F32)

    scale = scale_ref[...]
    a = 1.0 / pushed(p_ref, scale)
    a_ref[...] = a
    s_ref[...] = scale * pulled(p_ref, a)


def rhs_kernel(count, ratio, *refs):
    parts, (p_ref, scale_ref, gf_ref, g_ref, b_ref, cm_ref, m_ref, out_ref) = refs[:count], refs[count:]
    s = sum(q[...] for q in parts)
    b = ratio / s
    b_ref[...] = b
    cm_ref[...] = b * s

    scale = scale_ref[...]
    m = pushed(p_ref, scale * b)
    m_ref[...] = m
    out_ref[...] = g_ref[...] - b * scale * pulled(p_ref, gf_ref[...] / m)


def advance(parts, b, cm, dual, residual, direction):
    image = (1.0 + TAU) * cm * direction - b * sum(q[...] for q in parts)
    alpha = total(residual * residual) / total(direction * image)
    return alpha, dual + alpha * direction, residual - alpha * image


def cg_kernel(count, first, *refs):
    parts, refs = refs[:count], refs[count:]
    p_ref, scale_ref, a_ref, m_ref, b_ref, cm_ref = refs[:6]
    b = b_ref[...]
    if first:
        out = refs[6:]
        direction = sum(q[...] for q in parts)
        residual = direction
        dual = jnp.zeros_like(direction)
        mix = jnp.zeros(a_ref.shape, F32)
    else:
        dual_ref, res_ref, dir_ref, q_ref, mix_ref = refs[6:11]
        out = refs[11:]
        old = res_ref[...]
        before = dir_ref[...]
        alpha, dual, residual = advance(parts, b, cm_ref[...], dual_ref[...], old, before)
        direction = residual + total(residual * residual) / total(old * old) * before
        mix = mix_ref[...] + alpha * q_ref[...]
    dual_out, res_out, dir_out, q_out, mix_out, u_out = out
    dual_out[...] = dual
    res_out[...] = residual
    dir_out[...] = direction
    mix_out[...] = mix

    scale = scale_ref[...]
    q = pushed(p_ref, scale * b * direction)
    q_out[...] = q
    u_out[...] = scale * pulled(p_ref, a_ref[...] * q / m_ref[...])


def grad_kernel(count, group, *refs):
    parts, refs = refs[:count], refs[count:]
    me_ref, p_ref, scale_ref, a_ref, m_ref, b_ref, cm_ref, dual_ref, res_ref, dir_ref, q_ref, mix_ref = refs[:12]
    gf_ref, x_ref, yc_ref, srca_ref, srcb_ref, tgt_ref, step_ref = refs[12:19]
    wa_ref, wb_ref, va_ref, vb_ref, ad_ref, da_ref, db_ref = refs[19:]
    me = me_ref[0]
    replicas, _, ns = x_ref.shape
    features = srca_ref.shape[0]
    nt = tgt_ref.shape[2]
    b = b_ref[...]
    cm = cm_ref[...]
    old = res_ref[...]
    before = dir_ref[...]
    alpha, dual, residual = advance(parts, b, cm, dual_ref[...], old, before)
    norm = total(residual * residual)
    direction = residual + norm / total(old * old) * before
    a = a_ref[...]
    m = m_ref[...]
    mix = mix_ref[...] + alpha * q_ref[...]
    b = b * scale_ref[...]
    q = pushed(p_ref, b * direction)
    ad_ref[...] = down(a)
    da_ref[...] = down((gf_ref[...] / a - mix) / m)
    db_ref[...] = down(-q / m)
    step_ref[0:1, :] = jnp.broadcast_to(norm, (1, 128))
    step_ref[1:2, :] = jnp.broadcast_to(total((1.0 + TAU) * cm * direction * direction), (1, 128))
    taken = total(a * q * q / m)
    wide = b.shape[1]
    half = group * nt
    base = (me // group) * half

    def weigh(rows, source, bs, duals, dirs, outs):
        plan = source.astype(F32) * (ad_ref[rows, :] * bs)
        outs[0][...] = (plan * (da_ref[rows, :] + duals)).astype(BF16)
        outs[1][...] = (plan * (db_ref[rows, :] + dirs)).astype(BF16)

    for u in range(wide // 128):
        cs = slice(u * 128, (u + 1) * 128)
        weigh(slice(0, ns), p_ref[:ns, cs], b[:, cs], dual[:, cs], direction[:, cs], (wa_ref.at[:, cs], wb_ref.at[:, cs]))
    own = x_ref[0, :features, :].astype(F32)
    for w_ref, out_ref in ((wa_ref, srca_ref), (wb_ref, srcb_ref)):
        out = lax.dot_general(yc_ref[...], w_ref[...], NT, preferred_element_type=F32)
        out_ref[...] = 2.0 * (own * out[features : features + 1] - out[:features])

    b, dual, direction = [pick(v, me // group, half) for v in (b, dual, direction)]
    for u in range(half // 128):
        cs = slice(u * 128, (u + 1) * 128)
        cd = pl.ds(pl.multiple_of(base + u * 128, 128), 128)
        weigh(slice(None), p_ref[:, cd], b[:, cs], dual[:, cs], direction[:, cs], (va_ref.at[:, cs], vb_ref.at[:, cs]))
    mine = yc_ref[:features, pl.ds(pl.multiple_of(base, 128), half)].astype(F32)
    ones = jnp.ones((8, va_ref.shape[0]), BF16)
    for c, w_ref in enumerate((va_ref, vb_ref)):
        sums = jnp.zeros((features, half), F32)
        for k in range(replicas):
            rows = slice(k * ns, (k + 1) * ns)
            sums = sums + jnp.dot(x_ref[k, :features, :], w_ref[rows, :], preferred_element_type=F32)
        part = 2.0 * (mine * jnp.dot(ones, w_ref[...], preferred_element_type=F32)[:1] - sums)
        for k in range(group):
            slot = jnp.bitwise_xor(k, me % group)
            tgt_ref[slot, c * features : (c + 1) * features, :] = part[:, k * nt : (k + 1) * nt]
    for k in range(group):
        tgt_ref[k, 2 * features :, :] = jnp.broadcast_to(taken, (8, nt))


def last_kernel(count, *refs):
    parts, (srca_ref, srcb_ref, step_ref, src_ref, tgt_ref) = refs[:count], refs[count:]
    features = src_ref.shape[0]
    rows = sum(q[0] for q in parts)
    alpha = step_ref[0:1, 0:1] / (step_ref[1:2, 0:1] - rows[2 * features : 2 * features + 1, 0:1])
    src_ref[...] = srca_ref[...] + alpha * srcb_ref[...]
    tgt_ref[...] = rows[:features] + alpha * rows[features : 2 * features]


def pick(vector, index, size):
    out = vector[:, :size]
    for k in range(1, vector.shape[1] // size):
        out = jnp.where(index == k, vector[:, k * size : (k + 1) * size], out)
    return out


def call(kernel, operands, outs, scratch, smem=(), limit=24, alias={}):
    return pl.pallas_call(
        kernel,
        out_shape=outs,
        in_specs=[SMEM if i in smem else VMEM for i in range(len(operands))],
        out_specs=[VMEM] * len(outs),
        scratch_shapes=scratch,
        input_output_aliases=alias,
        compiler_params=pltpu.CompilerParams(vmem_limit_bytes=limit * 1024 * 1024),
    )(*operands)


def body(src_points, tgt_points, grad_f, grad_g):
    rows_axis, cols_axis = lax.axis_size("row"), lax.axis_size("col")
    devices = rows_axis * cols_axis
    features, ns = src_points.shape
    nt = tgt_points.shape[1]
    wide = devices * nt
    group = 2
    while group < devices and devices // group * ns * wide > ELEMENTS:
        group *= 2
    replicas = devices // group
    rows = replicas * ns
    row, col = lax.axis_index("row"), lax.axis_index("col")
    me = row * cols_axis + col
    me_ref = me.astype(jnp.int32).reshape(1)

    def swap(value, mask):
        return lax.ppermute(value, AXES, [(i, i ^ mask) for i in range(devices)])

    bits = [1 << i for i in range(1, group.bit_length() - 1)]
    stages = [[1]]
    for i in range(0, len(bits), 2):
        pair = bits[i : i + 2]
        stages.append(([pair[0] | pair[1]] if len(pair) == 2 else []) + pair[::-1])

    def exchange(value, combine):
        for stage in stages[:-1]:
            value = combine([value] + [swap(value, mask) for mask in stage])
        return [value] + [swap(value, mask) for mask in stages[-1]]

    x, y, gf = call(
        functools.partial(pack_kernel, cols_axis),
        (me_ref, src_points, tgt_points, grad_f.reshape(1, -1)),
        (
            jax.ShapeDtypeStruct((1, features, ns), BF16),
            jax.ShapeDtypeStruct((1, features, nt), BF16),
            jax.ShapeDtypeStruct((1, ns), F32),
        ),
        [],
        smem=(0,),
        limit=4,
    )
    mask = group
    while mask < devices:
        y = jnp.concatenate([y, swap(y, mask)])
        x = jnp.concatenate([x, swap(x, mask)])
        gf = jnp.concatenate([gf, swap(gf, mask)])
        mask *= 2
    for stage in stages[1:] + stages[:1]:
        sent = {0: y} | {mask // stage[-1]: swap(y, mask) for mask in stage}
        y = jnp.concatenate([sent[k] for k in range(len(sent))])
    gf = gf.reshape(1, rows)
    own = (jnp.arange(cols_axis)[None, :, None] == col) & (row % (group // cols_axis) == 0)
    g = jnp.where(own, grad_g.reshape(rows_axis, 1, nt), 0.0).reshape(1, wide)

    br = min(256, rows, ELEMENTS // 4 // wide)
    vec = jax.ShapeDtypeStruct((1, wide), F32)
    line = jax.ShapeDtypeStruct((1, rows), F32)
    acc = pltpu.VMEM((8, wide), F32)
    block = pltpu.VMEM((br, wide), F32)
    depth = -(-(3 * features + 8) // 128) * 128
    plan = jax.ShapeDtypeStruct((rows, wide), BF16)
    lhs, rhs, yc, p, r, lse = call(
        functools.partial(lse_kernel, group, br),
        (me_ref, x, y),
        (
            jax.ShapeDtypeStruct((rows, depth), BF16),
            jax.ShapeDtypeStruct((depth, wide), BF16),
            jax.ShapeDtypeStruct((features + 16, wide), BF16),
            plan,
            jax.ShapeDtypeStruct((rows, 128), F32),
            vec,
        ),
        [block, block, acc, acc],
        smem=(0,),
        limit=32,
    )

    def join(values):
        top = functools.reduce(jnp.maximum, values)
        return top + jnp.log2(sum(jnp.exp2(v - top) for v in values))

    parts = exchange(lse, join)
    count = len(parts)
    p, scale, a, s = call(
        functools.partial(plan_kernel, count, math.log2(ns / nt)),
        (*parts, lhs, rhs, r, p),
        (plan, vec, line, vec),
        [],
        alias={count + 3: 0},
    )
    parts = exchange(s, sum)
    b, cm, m, u = call(
        functools.partial(rhs_kernel, count, ns / nt),
        (*parts, p, scale, gf, g),
        (vec, vec, line, vec),
        [],
    )
    state = ()
    for step in range(CG - 1):
        parts = exchange(u, sum)
        *state, u = call(
            functools.partial(cg_kernel, count, step == 0),
            (*parts, p, scale, a, m, b, cm, *state),
            (vec, vec, vec, line, line, vec),
            [],
        )
    parts = exchange(u, sum)
    grad = jax.ShapeDtypeStruct((features, ns), F32)
    srca, srcb, part, scalars = call(
        functools.partial(grad_kernel, count, group),
        (*parts, me_ref, p, scale, a, m, b, cm, *state, gf, x, yc),
        (
            grad,
            grad,
            jax.ShapeDtypeStruct((group, 2 * features + 8, nt), F32),
            jax.ShapeDtypeStruct((8, 128), F32),
        ),
        [pltpu.VMEM((ns, wide), BF16)] * 2
        + [pltpu.VMEM((rows, group * nt), BF16)] * 2
        + [pltpu.VMEM((rows, 128), F32)] * 3,
        smem=(count,),
    )
    for stage in stages:
        size = len(stage) + 1
        part = part.reshape(part.shape[0] // size, size, *part.shape[1:])
        pieces = [part[:, 0]] + [swap(part[:, mask // stage[-1]], mask) for mask in stage]
        part = sum(pieces[1:], pieces[0]) if stage is not stages[-1] else part
    return call(
        functools.partial(last_kernel, len(pieces)),
        (*pieces, srca, srcb, scalars),
        (grad, jax.ShapeDtypeStruct((features, nt), F32)),
        [],
    )


def solution(mesh):
    in_specs = (P(None, ("row", "col")), P(None, ("col", "row")), P("row"), P("col"))
    out_specs = (P(None, ("row", "col")), P(None, ("col", "row")))

    return jax.shard_map(body, mesh=mesh, in_specs=in_specs, out_specs=out_specs, check_vma=False)
```

profile of v0, /device:TPU:0, one launch (start us, length us, event | category | flops | bytes accessed | tf_op | source)
XLA Modules:
  0.0 193.6 jit_solution(12989300817909716253)
XLA Ops:
  0.7 0.7 copy-done
  2.8 3.1 %collective-permute-start.2 = (bf16[1,64,128]{2,1,0:T(8,128)(2,1)S(1)}, bf16[1,64,128]{2,1,0:T(8,128)(2,1)S(1)}, u32[]{:S(2)}, u32[]{:S(2)}) collective-permute-start(bf16[1,64,128]{2,1,0:T(8,128)(2,1)S(1)} %get-tuple-element.36), channel_id=1, source_target_pairs={{0,8},{1,9},{2,10},{3,11},{4,12},{5,13},{6,14},{7,15},{8,0},{9,1},... | collective-permute-start | bytes 49160 | tf_op jit(solution)/shard_map/ppermute | solution.py:368
  6.0 1.9 %collective-permute-start.16 = (f32[1,256]{1,0:T(1,128)S(1)}, f32[1,256]{1,0:T(1,128)S(1)}, u32[]{:S(2)}, u32[]{:S(2)}) collective-permute-start(f32[1,256]{1,0:T(1,128)S(1)} %get-tuple-element.45), channel_id=1, source_target_pairs={{0,8},{1,9},{2,10},{3,11},{4,12},{5,13},{6,14},{7,15},{8,0},{9,1},... | collective-permute-start | bytes 3080 | tf_op jit(solution)/shard_map/ppermute | solution.py:368
  8.0 2.7 %collective-permute-start.3 = (bf16[2,64,128]{2,1,0:T(8,128)(2,1)S(1)}, bf16[2,64,128]{2,1,0:T(8,128)(2,1)S(1)}, u32[]{:S(2)}, u32[]{:S(2)}) collective-permute-start(bf16[2,64,128]{2,1,0:T(8,128)(2,1)S(1)} %pad_maximum_fusion.1), channel_id=1, source_target_pairs={{0,16},{1,17},{2,18},{3,19},{4,20},{5,21},{6,22},{7,23},{8,24},{9,... | collective-permute-start | bytes 98312 | tf_op jit(solution)/shard_map/ppermute | solution.py:368
  10.7 2.1 %collective-permute-done.3 = bf16[2,64,128]{2,1,0:T(8,128)(2,1)S(1)} collective-permute-done((bf16[2,64,128]{2,1,0:T(8,128)(2,1)S(1)}, bf16[2,64,128]{2,1,0:T(8,128)(2,1)S(1)}, u32[]{:S(2)}, u32[]{:S(2)}) %collective-permute-start.3) | collective-permute-done | bytes 32800 | tf_op jit(solution)/shard_map/ppermute | solution.py:368
  12.9 1.6 collective-permute-start.4
  14.6 1.5 collective-permute-start.5
  16.5 1.5 collective-permute-done.4
  18.0 0.9 collective-permute-done.5
  18.8 2.4 %collective-permute-done.6 = bf16[4,64,128]{2,1,0:T(8,128)(2,1)S(1)} collective-permute-done((bf16[4,64,128]{2,1,0:T(8,128)(2,1)S(1)}, bf16[4,64,128]{2,1,0:T(8,128)(2,1)S(1)}, u32[]{:S(2)}, u32[]{:S(2)}) %collective-permute-start.6) | collective-permute-done | bytes 65568 | tf_op jit(solution)/shard_map/ppermute | solution.py:368
  21.3 2.7 %collective-permute-start.1 = (bf16[2,64,256]{2,1,0:T(8,128)(2,1)S(1)}, bf16[2,64,256]{2,1,0:T(8,128)(2,1)S(1)}, u32[]{:S(2)}, u32[]{:S(2)}) collective-permute-start(bf16[2,64,256]{2,1,0:T(8,128)(2,1)S(1)} %pad_maximum_fusion), channel_id=1, source_target_pairs={{0,16},{1,17},{2,18},{3,19},{4,20},{5,21},{6,22},{7,23},{8,24},{9,... | collective-permute-start | bytes 196616 | tf_op jit(solution)/shard_map/ppermute | solution.py:368
  24.0 4.2 %collective-permute-done.1 = bf16[2,64,256]{2,1,0:T(8,128)(2,1)S(1)} collective-permute-done((bf16[2,64,256]{2,1,0:T(8,128)(2,1)S(1)}, bf16[2,64,256]{2,1,0:T(8,128)(2,1)S(1)}, u32[]{:S(2)}, u32[]{:S(2)}) %collective-permute-start.1) | collective-permute-done | bytes 65568 | tf_op jit(solution)/shard_map/ppermute | solution.py:368
  28.2 54.4 %shard_map.60 = (bf16[1024,256]{1,0:T(8,128)(2,1)S(1)}, bf16[256,4096]{1,0:T(8,128)(2,1)S(1)}, bf16[80,4096]{1,0:T(8,128)(2,1)S(1)}, bf16[1024,4096]{1,0:T(8,128...) custom-call(s32[1]{0:T(128)} %bitcast.me_ref.refs_4_, ...), custom_call_target="tpu_custom_call" | custom-call | tf_op jit(solution)/shard_map/pallas_call | solution.py:341
  82.7 1.2 collective-permute-done.8
  84.5 0.7 collective-permute-start.11
  85.3 2.2 %collective-permute-start.9 = (f32[1,4096]{1,0:T(1,128)S(1)}, f32[1,4096]{1,0:T(1,128)S(1)}, u32[]{:S(2)}, u32[]{:S(2)}) collective-permute-start(f32[1,4096]{1,0:T(1,128)S(1)} %multiply_add_fusion.refs_0_), channel_id=1, source_target_pairs={{0,6},{1,7},{2,4},{3,5},{4,2},{5,3},{6,0},{7,1},{8,14},{9,15},{10,... | collective-permute-start | bytes 49160 | tf_op jit(solution)/shard_map/ppermute | solution.py:368
  87.5 1.4 collective-permute-start.17
  88.9 1.0 collective-permute-done.9.refs_1_
  89.9 46.9 %shard_map.61 = (bf16[1024,4096]{1,0:T(8,128)(2,1)S(1)}, f32[1,4096]{1,0:T(1,128)S(1)}, f32[1,1024]{1,0:T(1,128)S(1)}, f32[1,4096]{1,0:T(1,128)S(1)}) custom-call(f32[1,4096]{1,0:T(1,128)S(1)} %multiply_add_fusion.refs_0_, f32[1,4096]{1,0:T(1,128)S(1)} %collective-permute-done.9.refs_1_, ...), custom_call_target="tpu_custom_call", output_to_operand_aliasing={{0}: (7, {})} | custom-call | tf_op jit(solution)/shard_map/pallas_call | solution.py:341
  136.9 1.1 collective-permute-done.12
  138.0 2.3 %collective-permute-start.13 = (f32[1,4096]{1,0:T(1,128)S(1)}, f32[1,4096]{1,0:T(1,128)S(1)}, u32[]{:S(2)}, u32[]{:S(2)}) collective-permute-start(f32[1,4096]{1,0:T(1,128)S(1)} %add.31.refs_0_), channel_id=1, source_target_pairs={{0,6},{1,7},{2,4},{3,5},{4,2},{5,3},{6,0},{7,1},{8,14},{9,15},{10,... | collective-permute-start | bytes 49160 | tf_op jit(solution)/shard_map/ppermute | solution.py:368
  141.6 1.1 collective-permute-done.13.refs_1_
  142.8 1.3 collective-permute-done.14.refs_2_
  144.6 3.5 %shard_map.62 = (f32[1,4096]{1,0:T(1,128)S(1)}, f32[1,4096]{1,0:T(1,128)S(1)}, f32[1,1024]{1,0:T(1,128)S(1)}, f32[1,4096]{1,0:T(1,128)S(1)}) custom-call(f32[1,4096]{1,0:T(1,128)S(1)} %add.31.refs_0_, f32[1,4096]{1,0:T(1,128)S(1)} %collective-permute-done.13.refs_1_, f32[1,4096]{1,0:T(1,128)S(1)} %collective-permute-done.14.refs_2_, ...), custom_call_target="tpu_custom_call" | custom-call | tf_op jit(solution)/shard_map/pallas_call | solution.py:341
  148.2 1.2 collective-permute-done.18
  149.4 1.5 collective-permute-start.19
  150.9 0.8 collective-permute-start.20
  151.6 1.3 collective-permute-start.21
  152.9 1.2 collective-permute-done.19.refs_1_
  154.6 0.8 collective-permute-done.21.refs_3_
  155.4 3.5 %shard_map.63 = (f32[1,4096]{1,0:T(1,128)S(1)}, f32[1,4096]{1,0:T(1,128)S(1)}, f32[1,4096]{1,0:T(1,128)S(1)}, f32[1,1024]{1,0:T(1,128)S(1)}, f32[1,1024]{1,0:T(1,128)S(1)}, /*index=5*/f32[1,4096]{1,0:T(1,128)S(1)}) custom-call(f32[1,4096]{1,0:T(1,128)S(1)} %add.33.refs_0_, f32[1,4096]{1,0:T(1,128)S(1)} %collective-permute-done.19.refs_1_, ...), custom_call_target="tpu_custom_call" | custom-call | tf_op jit(solution)/shard_map/pallas_call | solution.py:341
  159.0 1.2 collective-permute-done.22
  160.2 2.3 %collective-permute-start.23 = (f32[1,4096]{1,0:T(1,128)S(1)}, f32[1,4096]{1,0:T(1,128)S(1)}, u32[]{:S(2)}, u32[]{:S(2)}) collective-permute-start(f32[1,4096]{1,0:T(1,128)S(1)} %add.34.refs_0_), channel_id=1, source_target_pairs={{0,6},{1,7},{2,4},{3,5},{4,2},{5,3},{6,0},{7,1},{8,14},{9,15},{10,... | collective-permute-start | bytes 49160 | tf_op jit(solution)/shard_map/ppermute | solution.py:368
  163.0 0.7 collective-permute-start.25
  163.7 1.1 collective-permute-done.23.refs_1_
  164.9 1.3 collective-permute-done.24.refs_2_
  166.7 3.7 %shard_map.64 = (f32[1,4096]{1,0:T(1,128)S(1)}, f32[1,4096]{1,0:T(1,128)S(1)}, f32[1,4096]{1,0:T(1,128)S(1)}, f32[1,1024]{1,0:T(1,128)S(1)}, f32[1,1024]{1,0:T(1,128)S(1)}, /*index=5*/f32[1,4096]{1,0:T(1,128)S(1)}) custom-call(f32[1,4096]{1,0:T(1,128)S(1)} %add.34.refs_0_, f32[1,4096]{1,0:T(1,128)S(1)} %collective-permute-done.23.refs_1_, ...), custom_call_target="tpu_custom_call" | custom-call | tf_op jit(solution)/shard_map/pallas_call | solution.py:341
  170.5 1.2 collective-permute-done.26
  171.7 1.5 collective-permute-start.27
  173.2 0.8 collective-permute-start.28
  174.0 1.3 collective-permute-start.29
  175.3 1.2 collective-permute-done.27.refs_1_
  177.0 0.8 collective-permute-done.29.refs_3_
  177.7 6.4 %shard_map.65 = (f32[64,256]{1,0:T(8,128)S(1)}, f32[64,256]{1,0:T(8,128)S(1)}, f32[8,136,128]{2,1,0:T(8,128)S(1)}, f32[8,128]{1,0:T(8,128)S(1)}) custom-call(f32[1,4096]{1,0:T(1,128)S(1)} %add.35.refs_0_, f32[1,4096]{1,0:T(1,128)S(1)} %collective-permute-done.27.refs_1_, f32[1,4096]{1,0:T(1,128)S(1)} %collective-permute-done.28.refs_2_, ...), custom_call_target="tpu_custom_call" | custom-call | tf_op jit(solution)/shard_map/pallas_call | solution.py:341
  184.2 1.5 collective-permute-done.30
  185.8 2.3 %collective-permute-start.31 = (f32[1,136,128]{2,1,0:T(8,128)S(1)}, f32[1,136,128]{2,1,0:T(8,128)S(1)}, u32[]{:S(2)}, u32[]{:S(2)}) collective-permute-start(f32[1,136,128]{2,1,0:T(8,128)S(1)} %get-tuple-element.70), channel_id=1, source_target_pairs={{0,6},{1,7},{2,4},{3,5},{4,2},{5,3},{6,0},{7,1},{8,14},{9,15},{10,... | collective-permute-start | bytes 208904 | tf_op jit(solution)/shard_map/ppermute | solution.py:368
  189.4 2.3 %collective-permute-done.31.refs_1_ = f32[1,136,128]{2,1,0:T(8,128)S(1)} collective-permute-done((f32[1,136,128]{2,1,0:T(8,128)S(1)}, f32[1,136,128]{2,1,0:T(8,128)S(1)}, u32[]{:S(2)}, u32[]{:S(2)}) %collective-permute-start.31) | collective-permute-done | bytes 69664 | tf_op jit(solution)/shard_map/ppermute | solution.py:368
  191.7 0.7 collective-permute-done.32.refs_2_
  (61 shorter events, 9.8 us)
Async XLA Ops:
  0.6 136.2 %copy-start.3 = (f32[1024]{0:T(1024)S(1)}, f32[1024]{0:T(1024)}, u32[]{:S(2)}) copy-start(f32[1024]{0:T(1024)} %param.7) | copy-start | bytes 12292
  0.6 0.8 copy-start
  1.4 0.7 copy-start.1
  2.1 0.7 copy-start.2
  2.8 5.2 %collective-permute-start.2 = (bf16[1,64,128]{2,1,0:T(8,128)(2,1)S(1)}, bf16[1,64,128]{2,1,0:T(8,128)(2,1)S(1)}, u32[]{:S(2)}, u32[]{:S(2)}) collective-permute-start(bf16[1,64,128]{2,1,0:T(8,128)(2,1)S(1)} %get-tuple-element.36), channel_id=1, source_target_pairs={{0,8},{1,9},{2,10},{3,11},{4,12},{5,13},{6,14},{7,15},{8,0},{9,1},... | collective-permute-start | bytes 49160 | tf_op jit(solution)/shard_map/ppermute | solution.py:368
  5.9 15.4 %collective-permute-start = (bf16[1,64,256]{2,1,0:T(8,128)(2,1)S(1)}, bf16[1,64,256]{2,1,0:T(8,128)(2,1)S(1)}, u32[]{:S(2)}, u32[]{:S(2)}) collective-permute-start(bf16[1,64,256]{2,1,0:T(8,128)(2,1)S(1)} %get-tuple-element.35), channel_id=1, source_target_pairs={{0,8},{1,9},{2,10},{3,11},{4,12},{5,13},{6,14},{7,15},{8,0},{9,1},... | collective-permute-start | bytes 98312 | tf_op jit(solution)/shard_map/ppermute | solution.py:368
  6.0 81.5 %collective-permute-start.16 = (f32[1,256]{1,0:T(1,128)S(1)}, f32[1,256]{1,0:T(1,128)S(1)}, u32[]{:S(2)}, u32[]{:S(2)}) collective-permute-start(f32[1,256]{1,0:T(1,128)S(1)} %get-tuple-element.45), channel_id=1, source_target_pairs={{0,8},{1,9},{2,10},{3,11},{4,12},{5,13},{6,14},{7,15},{8,0},{9,1},... | collective-permute-start | bytes 3080 | tf_op jit(solution)/shard_map/ppermute | solution.py:368
  8.0 4.9 %collective-permute-start.3 = (bf16[2,64,128]{2,1,0:T(8,128)(2,1)S(1)}, bf16[2,64,128]{2,1,0:T(8,128)(2,1)S(1)}, u32[]{:S(2)}, u32[]{:S(2)}) collective-permute-start(bf16[2,64,128]{2,1,0:T(8,128)(2,1)S(1)} %pad_maximum_fusion.1), channel_id=1, source_target_pairs={{0,16},{1,17},{2,18},{3,19},{4,20},{5,21},{6,22},{7,23},{8,24},{9,... | collective-permute-start | bytes 98312 | tf_op jit(solution)/shard_map/ppermute | solution.py:368
  12.9 5.0 %collective-permute-start.4 = (bf16[4,64,128]{2,1,0:T(8,128)(2,1)S(1)}, bf16[4,64,128]{2,1,0:T(8,128)(2,1)S(1)}, u32[]{:S(2)}, u32[]{:S(2)}) collective-permute-start(bf16[4,64,128]{2,1,0:T(8,128)(2,1)S(1)} %get-tuple-element.80), channel_id=1, source_target_pairs={{0,2},{1,3},{2,0},{3,1},{4,6},{5,7},{6,4},{7,5},{8,10},{9,11},{10,... | collective-permute-start | bytes 196616 | tf_op jit(solution)/shard_map/ppermute | solution.py:368
  14.6 4.3 %collective-permute-start.5 = (bf16[4,64,128]{2,1,0:T(8,128)(2,1)S(1)}, bf16[4,64,128]{2,1,0:T(8,128)(2,1)S(1)}, u32[]{:S(2)}, u32[]{:S(2)}) collective-permute-start(bf16[4,64,128]{2,1,0:T(8,128)(2,1)S(1)} %get-tuple-element.80), channel_id=1, source_target_pairs={{0,4},{1,5},{2,6},{3,7},{4,0},{5,1},{6,2},{7,3},{8,12},{9,13},{10,... | collective-permute-start | bytes 196616 | tf_op jit(solution)/shard_map/ppermute | solution.py:368
  16.0 5.2 %collective-permute-start.6 = (bf16[4,64,128]{2,1,0:T(8,128)(2,1)S(1)}, bf16[4,64,128]{2,1,0:T(8,128)(2,1)S(1)}, u32[]{:S(2)}, u32[]{:S(2)}) collective-permute-start(bf16[4,64,128]{2,1,0:T(8,128)(2,1)S(1)} %get-tuple-element.80), channel_id=1, source_target_pairs={{0,6},{1,7},{2,4},{3,5},{4,2},{5,3},{6,0},{7,1},{8,14},{9,15},{10,... | collective-permute-start | bytes 196616 | tf_op jit(solution)/shard_map/ppermute | solution.py:368
  21.2 7.0 %collective-permute-start.7 = (bf16[16,64,128]{2,1,0:T(8,128)(2,1)S(1)}, bf16[16,64,128]{2,1,0:T(8,128)(2,1)S(1)}, u32[]{:S(2)}, u32[]{:S(2)}) collective-permute-start(bf16[16,64,128]{2,1,0:T(8,128)(2,1)S(1)} %get-tuple-element.72), channel_id=1, source_target_pairs={{0,1},{1,0},{2,3},{3,2},{4,5},{5,4},{6,7},{7,6},{8,9},{9,8},{10,11... | collective-permute-start | bytes 786440 | tf_op jit(solution)/shard_map/ppermute | solution.py:368
  21.3 6.8 %collective-permute-start.1 = (bf16[2,64,256]{2,1,0:T(8,128)(2,1)S(1)}, bf16[2,64,256]{2,1,0:T(8,128)(2,1)S(1)}, u32[]{:S(2)}, u32[]{:S(2)}) collective-permute-start(bf16[2,64,256]{2,1,0:T(8,128)(2,1)S(1)} %pad_maximum_fusion), channel_id=1, source_target_pairs={{0,16},{1,17},{2,18},{3,19},{4,20},{5,21},{6,22},{7,23},{8,24},{9,... | collective-permute-start | bytes 196616 | tf_op jit(solution)/shard_map/ppermute | solution.py:368
  82.6 1.2 collective-permute-start.8
  83.9 4.9 %collective-permute-start.10 = (f32[1,4096]{1,0:T(1,128)S(1)}, f32[1,4096]{1,0:T(1,128)S(1)}, u32[]{:S(2)}, u32[]{:S(2)}) collective-permute-start(f32[1,4096]{1,0:T(1,128)S(1)} %multiply_add_fusion.refs_0_), channel_id=1, source_target_pairs={{0,4},{1,5},{2,6},{3,7},{4,0},{5,1},{6,2},{7,3},{8,12},{9,13},{10,... | collective-permute-start | bytes 49160 | tf_op jit(solution)/shard_map/ppermute | solution.py:368
  84.5 4.3 %collective-permute-start.11 = (f32[1,4096]{1,0:T(1,128)S(1)}, f32[1,4096]{1,0:T(1,128)S(1)}, u32[]{:S(2)}, u32[]{:S(2)}) collective-permute-start(f32[1,4096]{1,0:T(1,128)S(1)} %multiply_add_fusion.refs_0_), channel_id=1, source_target_pairs={{0,2},{1,3},{2,0},{3,1},{4,6},{5,7},{6,4},{7,5},{8,10},{9,11},{10,... | collective-permute-start | bytes 49160 | tf_op jit(solution)/shard_map/ppermute | solution.py:368
  85.3 4.6 %collective-permute-start.9 = (f32[1,4096]{1,0:T(1,128)S(1)}, f32[1,4096]{1,0:T(1,128)S(1)}, u32[]{:S(2)}, u32[]{:S(2)}) collective-permute-start(f32[1,4096]{1,0:T(1,128)S(1)} %multiply_add_fusion.refs_0_), channel_id=1, source_target_pairs={{0,6},{1,7},{2,4},{3,5},{4,2},{5,3},{6,0},{7,1},{8,14},{9,15},{10,... | collective-permute-start | bytes 49160 | tf_op jit(solution)/shard_map/ppermute | solution.py:368
  87.5 54.1 %collective-permute-start.17 = (f32[2,256]{1,0:T(2,128)S(1)}, f32[2,256]{1,0:T(2,128)S(1)}, u32[]{:S(2)}, u32[]{:S(2)}) collective-permute-start(f32[2,256]{1,0:T(2,128)S(1)} %pad_maximum_fusion.2), channel_id=1, source_target_pairs={{0,16},{1,17},{2,18},{3,19},{4,20},{5,21},{6,22},{7,23},{8,24},{9,... | collective-permute-start | bytes 6152 | tf_op jit(solution)/shard_map/ppermute | solution.py:368
  136.8 1.2 collective-permute-start.12
  138.0 4.7 %collective-permute-start.13 = (f32[1,4096]{1,0:T(1,128)S(1)}, f32[1,4096]{1,0:T(1,128)S(1)}, u32[]{:S(2)}, u32[]{:S(2)}) collective-permute-start(f32[1,4096]{1,0:T(1,128)S(1)} %add.31.refs_0_), channel_id=1, source_target_pairs={{0,6},{1,7},{2,4},{3,5},{4,2},{5,3},{6,0},{7,1},{8,14},{9,15},{10,... | collective-permute-start | bytes 49160 | tf_op jit(solution)/shard_map/ppermute | solution.py:368
  140.3 3.7 %collective-permute-start.14 = (f32[1,4096]{1,0:T(1,128)S(1)}, f32[1,4096]{1,0:T(1,128)S(1)}, u32[]{:S(2)}, u32[]{:S(2)}) collective-permute-start(f32[1,4096]{1,0:T(1,128)S(1)} %add.31.refs_0_), channel_id=1, source_target_pairs={{0,4},{1,5},{2,6},{3,7},{4,0},{5,1},{6,2},{7,3},{8,12},{9,13},{10,... | collective-permute-start | bytes 49160 | tf_op jit(solution)/shard_map/ppermute | solution.py:368
  140.9 3.7 %collective-permute-start.15 = (f32[1,4096]{1,0:T(1,128)S(1)}, f32[1,4096]{1,0:T(1,128)S(1)}, u32[]{:S(2)}, u32[]{:S(2)}) collective-permute-start(f32[1,4096]{1,0:T(1,128)S(1)} %add.31.refs_0_), channel_id=1, source_target_pairs={{0,2},{1,3},{2,0},{3,1},{4,6},{5,7},{6,4},{7,5},{8,10},{9,11},{10,... | collective-permute-start | bytes 49160 | tf_op jit(solution)/shard_map/ppermute | solution.py:368
  148.1 1.2 collective-permute-start.18
  149.4 4.8 %collective-permute-start.19 = (f32[1,4096]{1,0:T(1,128)S(1)}, f32[1,4096]{1,0:T(1,128)S(1)}, u32[]{:S(2)}, u32[]{:S(2)}) collective-permute-start(f32[1,4096]{1,0:T(1,128)S(1)} %add.33.refs_0_), channel_id=1, source_target_pairs={{0,6},{1,7},{2,4},{3,5},{4,2},{5,3},{6,0},{7,1},{8,14},{9,15},{10,... | collective-permute-start | bytes 49160 | tf_op jit(solution)/shard_map/ppermute | solution.py:368
  150.9 3.7 %collective-permute-start.20 = (f32[1,4096]{1,0:T(1,128)S(1)}, f32[1,4096]{1,0:T(1,128)S(1)}, u32[]{:S(2)}, u32[]{:S(2)}) collective-permute-start(f32[1,4096]{1,0:T(1,128)S(1)} %add.33.refs_0_), channel_id=1, source_target_pairs={{0,4},{1,5},{2,6},{3,7},{4,0},{5,1},{6,2},{7,3},{8,12},{9,13},{10,... | collective-permute-start | bytes 49160 | tf_op jit(solution)/shard_map/ppermute | solution.py:368
  151.6 3.7 %collective-permute-start.21 = (f32[1,4096]{1,0:T(1,128)S(1)}, f32[1,4096]{1,0:T(1,128)S(1)}, u32[]{:S(2)}, u32[]{:S(2)}) collective-permute-start(f32[1,4096]{1,0:T(1,128)S(1)} %add.33.refs_0_), channel_id=1, source_target_pairs={{0,2},{1,3},{2,0},{3,1},{4,6},{5,7},{6,4},{7,5},{8,10},{9,11},{10,... | collective-permute-start | bytes 49160 | tf_op jit(solution)/shard_map/ppermute | solution.py:368
  158.9 1.2 collective-permute-start.22
  160.2 4.7 %collective-permute-start.23 = (f32[1,4096]{1,0:T(1,128)S(1)}, f32[1,4096]{1,0:T(1,128)S(1)}, u32[]{:S(2)}, u32[]{:S(2)}) collective-permute-start(f32[1,4096]{1,0:T(1,128)S(1)} %add.34.refs_0_), channel_id=1, source_target_pairs={{0,6},{1,7},{2,4},{3,5},{4,2},{5,3},{6,0},{7,1},{8,14},{9,15},{10,... | collective-permute-start | bytes 49160 | tf_op jit(solution)/shard_map/ppermute | solution.py:368
  162.4 3.7 %collective-permute-start.24 = (f32[1,4096]{1,0:T(1,128)S(1)}, f32[1,4096]{1,0:T(1,128)S(1)}, u32[]{:S(2)}, u32[]{:S(2)}) collective-permute-start(f32[1,4096]{1,0:T(1,128)S(1)} %add.34.refs_0_), channel_id=1, source_target_pairs={{0,4},{1,5},{2,6},{3,7},{4,0},{5,1},{6,2},{7,3},{8,12},{9,13},{10,... | collective-permute-start | bytes 49160 | tf_op jit(solution)/shard_map/ppermute | solution.py:368
  163.0 3.7 %collective-permute-start.25 = (f32[1,4096]{1,0:T(1,128)S(1)}, f32[1,4096]{1,0:T(1,128)S(1)}, u32[]{:S(2)}, u32[]{:S(2)}) collective-permute-start(f32[1,4096]{1,0:T(1,128)S(1)} %add.34.refs_0_), channel_id=1, source_target_pairs={{0,2},{1,3},{2,0},{3,1},{4,6},{5,7},{6,4},{7,5},{8,10},{9,11},{10,... | collective-permute-start | bytes 49160 | tf_op jit(solution)/shard_map/ppermute | solution.py:368
  170.5 1.2 collective-permute-start.26
  171.7 4.8 %collective-permute-start.27 = (f32[1,4096]{1,0:T(1,128)S(1)}, f32[1,4096]{1,0:T(1,128)S(1)}, u32[]{:S(2)}, u32[]{:S(2)}) collective-permute-start(f32[1,4096]{1,0:T(1,128)S(1)} %add.35.refs_0_), channel_id=1, source_target_pairs={{0,6},{1,7},{2,4},{3,5},{4,2},{5,3},{6,0},{7,1},{8,14},{9,15},{10,... | collective-permute-start | bytes 49160 | tf_op jit(solution)/shard_map/ppermute | solution.py:368
  173.2 3.7 %collective-permute-start.28 = (f32[1,4096]{1,0:T(1,128)S(1)}, f32[1,4096]{1,0:T(1,128)S(1)}, u32[]{:S(2)}, u32[]{:S(2)}) collective-permute-start(f32[1,4096]{1,0:T(1,128)S(1)} %add.35.refs_0_), channel_id=1, source_target_pairs={{0,4},{1,5},{2,6},{3,7},{4,0},{5,1},{6,2},{7,3},{8,12},{9,13},{10,... | collective-permute-start | bytes 49160 | tf_op jit(solution)/shard_map/ppermute | solution.py:368
  174.0 3.7 %collective-permute-start.29 = (f32[1,4096]{1,0:T(1,128)S(1)}, f32[1,4096]{1,0:T(1,128)S(1)}, u32[]{:S(2)}, u32[]{:S(2)}) collective-permute-start(f32[1,4096]{1,0:T(1,128)S(1)} %add.35.refs_0_), channel_id=1, source_target_pairs={{0,2},{1,3},{2,0},{3,1},{4,6},{5,7},{6,4},{7,5},{8,10},{9,11},{10,... | collective-permute-start | bytes 49160 | tf_op jit(solution)/shard_map/ppermute | solution.py:368
  184.1 1.6 collective-permute-start.30
  185.8 5.9 %collective-permute-start.31 = (f32[1,136,128]{2,1,0:T(8,128)S(1)}, f32[1,136,128]{2,1,0:T(8,128)S(1)}, u32[]{:S(2)}, u32[]{:S(2)}) collective-permute-start(f32[1,136,128]{2,1,0:T(8,128)S(1)} %get-tuple-element.70), channel_id=1, source_target_pairs={{0,6},{1,7},{2,4},{3,5},{4,2},{5,3},{6,0},{7,1},{8,14},{9,15},{10,... | collective-permute-start | bytes 208904 | tf_op jit(solution)/shard_map/ppermute | solution.py:368
  188.1 4.3 %collective-permute-start.32 = (f32[1,136,128]{2,1,0:T(8,128)S(1)}, f32[1,136,128]{2,1,0:T(8,128)S(1)}, u32[]{:S(2)}, u32[]{:S(2)}) collective-permute-start(f32[1,136,128]{2,1,0:T(8,128)S(1)} %get-tuple-element.69), channel_id=1, source_target_pairs={{0,4},{1,5},{2,6},{3,7},{4,0},{5,1},{6,2},{7,3},{8,12},{9,13},{10,... | collective-permute-start | bytes 208904 | tf_op jit(solution)/shard_map/ppermute | solution.py:368
  188.6 4.3 %collective-permute-start.33 = (f32[1,136,128]{2,1,0:T(8,128)S(1)}, f32[1,136,128]{2,1,0:T(8,128)S(1)}, u32[]{:S(2)}, u32[]{:S(2)}) collective-permute-start(f32[1,136,128]{2,1,0:T(8,128)S(1)} %get-tuple-element.68), channel_id=1, source_target_pairs={{0,2},{1,3},{2,0},{3,1},{4,6},{5,7},{6,4},{7,5},{8,10},{9,11},{10,... | collective-permute-start | bytes 208904 | tf_op jit(solution)/shard_map/ppermute | solution.py:368
where the time goes:
time: 194 us
  Pallas kernels  119 us (61%)
  starting transfers between devices  37.3 us (19%)
  waiting for transfers between devices  33.8 us (17%)
  local copies, waits for them, and re-layouts  2.38 us (1%)
    pallas_call x8, Pallas kernels, call(): pl.pallas_call(kernel, out_shape=outs, in_specs=[SMEM if i in smem else V...  119 us
    ppermute x34, starting transfers between devices, swap(): return lax.ppermute(value, AXES, [(i, i ^ mask) for i in range(devices)])  37.3 us
    ppermute x34, waiting for transfers between devices, swap(): return lax.ppermute(value, AXES, [(i, i ^ mask) for i in range(devices)])  33.8 us
  transfers between devices with their start and end apart: 34, of which 27 were waited for; matrix products, arithmetic and copies ran while one was open for 0% of the time, Pallas kernels for 52%

commit v1 on v0

--- a/solution.py
+++ b/solution.py
@@ -392,14 +392,12 @@
     )
     mask = group
     while mask < devices:
-        y = jnp.concatenate([y, swap(y, mask)])
-        x = jnp.concatenate([x, swap(x, mask)])
-        gf = jnp.concatenate([gf, swap(gf, mask)])
+        y = jnp.concatenate([y, swap(y if mask > group else tgt_points[None], mask)])
+        x = jnp.concatenate([x, swap(x if mask > group else src_points[None], mask)])
         mask *= 2
     for stage in stages[1:] + stages[:1]:
         sent = {0: y} | {mask // stage[-1]: swap(y, mask) for mask in stage}
         y = jnp.concatenate([sent[k] for k in range(len(sent))])
-    gf = gf.reshape(1, rows)
     own = (jnp.arange(cols_axis)[None, :, None] == col) & (row % (group // cols_axis) == 0)
     g = jnp.where(own, grad_g.reshape(rows_axis, 1, nt), 0.0).reshape(1, wide)
 
@@ -425,6 +423,13 @@
         smem=(0,),
         limit=32,
     )
+
+    lse, gf = lax.optimization_barrier((lse, gf))
+    mask = group
+    while mask < devices:
+        gf = jnp.concatenate([gf, swap(gf, mask)])
+        mask *= 2
+    gf = gf.reshape(1, rows)
 
     def join(values):
         top = functools.reduce(jnp.maximum, values)

time: 194 us -> 193 us (level)
  transfers between devices with their start and end apart: 34 -> 34, of which waited for: 27 -> 26; matrix products, arithmetic and copies ran while one was open for 0% -> 0% of each run, Pallas kernels for 52% -> 24%
where the time goes in v1:
time: 193 us
  Pallas kernels  119 us (62%)
  starting transfers between devices  35.8 us (19%)
  waiting for transfers between devices  34.8 us (18%)
  local copies, waits for them, and re-layouts  2.38 us (1%)
    pallas_call x8, Pallas kernels, call(): pl.pallas_call(kernel, out_shape=outs, in_specs=[SMEM if i in smem else V...  119 us
    ppermute x34, starting transfers between devices, swap(): return lax.ppermute(value, AXES, [(i, i ^ mask) for i in range(devices)])  35.8 us
    ppermute x34, waiting for transfers between devices, swap(): return lax.ppermute(value, AXES, [(i, i ^ mask) for i in range(devices)])  34.8 us
  transfers between devices with their start and end apart: 34, of which 26 were waited for; matrix products, arithmetic and copies ran while one was open for 0% of the time, Pallas kernels for 24%

profile of v1, /device:TPU:0, one launch (start us, length us, event | category | flops | bytes accessed | tf_op | source)
XLA Modules:
  0.0 193.2 jit_solution(458389783940204041)
XLA Ops:
  0.6 3.1 %collective-permute-start = (bf16[1,64,256]{2,1,0:T(8,128)(2,1)}, bf16[1,64,256]{2,1,0:T(8,128)(2,1)S(1)}, u32[]{:S(2)}, u32[]{:S(2)}) collective-permute-start(bf16[1,64,256]{2,1,0:T(8,128)(2,1)} %bitcast.38), channel_id=1, source_target_pairs={{0,8},{1,9},{2,10},{3,11},{4,12},{5,13},{6,14},{7,15},{8,0},{9,1},... | collective-permute-start | bytes 98312 | tf_op jit(solution)/shard_map/ppermute | solution.py:368
  6.0 1.7 collective-permute-done.2
  7.7 2.6 %collective-permute-start.3 = (bf16[2,64,128]{2,1,0:T(8,128)(2,1)S(1)}, bf16[2,64,128]{2,1,0:T(8,128)(2,1)S(1)}, u32[]{:S(2)}, u32[]{:S(2)}) collective-permute-start(bf16[2,64,128]{2,1,0:T(8,128)(2,1)S(1)} %pad_maximum_fusion.1), channel_id=1, source_target_pairs={{0,16},{1,17},{2,18},{3,19},{4,20},{5,21},{6,22},{7,23},{8,24},{9,... | collective-permute-start | bytes 98312 | tf_op jit(solution)/shard_map/ppermute | solution.py:368
  10.3 2.4 %collective-permute-done.3 = bf16[2,64,128]{2,1,0:T(8,128)(2,1)S(1)} collective-permute-done((bf16[2,64,128]{2,1,0:T(8,128)(2,1)S(1)}, bf16[2,64,128]{2,1,0:T(8,128)(2,1)S(1)}, u32[]{:S(2)}, u32[]{:S(2)}) %collective-permute-start.3) | collective-permute-done | bytes 32800 | tf_op jit(solution)/shard_map/ppermute | solution.py:368
  12.7 1.7 collective-permute-start.4
  14.4 1.5 collective-permute-start.5
  16.3 1.5 collective-permute-done.4
  17.8 0.9 collective-permute-done.5
  18.7 2.4 %collective-permute-done.6 = bf16[4,64,128]{2,1,0:T(8,128)(2,1)S(1)} collective-permute-done((bf16[4,64,128]{2,1,0:T(8,128)(2,1)S(1)}, bf16[4,64,128]{2,1,0:T(8,128)(2,1)S(1)}, u32[]{:S(2)}, u32[]{:S(2)}) %collective-permute-start.6) | collective-permute-done | bytes 65568 | tf_op jit(solution)/shard_map/ppermute | solution.py:368
  21.2 2.4 %collective-permute-start.1 = (bf16[2,64,256]{2,1,0:T(8,128)(2,1)S(1)}, bf16[2,64,256]{2,1,0:T(8,128)(2,1)S(1)}, u32[]{:S(2)}, u32[]{:S(2)}) collective-permute-start(bf16[2,64,256]{2,1,0:T(8,128)(2,1)S(1)} %pad_maximum_fusion), channel_id=1, source_target_pairs={{0,16},{1,17},{2,18},{3,19},{4,20},{5,21},{6,22},{7,23},{8,24},{9,... | collective-permute-start | bytes 196616 | tf_op jit(solution)/shard_map/ppermute | solution.py:368
  23.6 4.1 %collective-permute-done.1 = bf16[2,64,256]{2,1,0:T(8,128)(2,1)S(1)} collective-permute-done((bf16[2,64,256]{2,1,0:T(8,128)(2,1)S(1)}, bf16[2,64,256]{2,1,0:T(8,128)(2,1)S(1)}, u32[]{:S(2)}, u32[]{:S(2)}) %collective-permute-start.1) | collective-permute-done | bytes 65568 | tf_op jit(solution)/shard_map/ppermute | solution.py:368
  27.8 54.4 %shard_map.60 = (bf16[1024,256]{1,0:T(8,128)(2,1)S(1)}, bf16[256,4096]{1,0:T(8,128)(2,1)S(1)}, bf16[80,4096]{1,0:T(8,128)(2,1)S(1)}, bf16[1024,4096]{1,0:T(8,128...) custom-call(s32[1]{0:T(128)} %bitcast.me_ref.refs_4_, ...), custom_call_target="tpu_custom_call" | custom-call | tf_op jit(solution)/shard_map/pallas_call | solution.py:341
  82.3 1.1 collective-permute-done.8
  83.4 0.8 collective-permute-start.9
  84.2 1.3 collective-permute-start.10
  85.5 1.5 collective-permute-start.11
  87.0 2.1 %collective-permute-start.17 = (f32[2,256]{1,0:T(2,128)S(1)}, f32[2,256]{1,0:T(2,128)S(1)}, u32[]{:S(2)}, u32[]{:S(2)}) collective-permute-start(f32[2,256]{1,0:T(2,128)S(1)} %pad_maximum_fusion.2), channel_id=1, source_target_pairs={{0,16},{1,17},{2,18},{3,19},{4,20},{5,21},{6,22},{7,23},{8,24},{9,... | collective-permute-start | bytes 6152 | tf_op jit(solution)/shard_map/ppermute | solution.py:368
  89.2 46.9 %shard_map.61 = (bf16[1024,4096]{1,0:T(8,128)(2,1)S(1)}, f32[1,4096]{1,0:T(1,128)S(1)}, f32[1,1024]{1,0:T(1,128)S(1)}, f32[1,4096]{1,0:T(1,128)S(1)}) custom-call(f32[1,4096]{1,0:T(1,128)S(1)} %multiply_add_fusion.refs_0_, f32[1,4096]{1,0:T(1,128)S(1)} %collective-permute-done.9.refs_1_, ...), custom_call_target="tpu_custom_call", output_to_operand_aliasing={{0}: (7, {})} | custom-call | tf_op jit(solution)/shard_map/pallas_call | solution.py:341
  136.2 1.1 collective-permute-done.12
  137.4 1.5 collective-permute-start.13
  138.9 1.5 collective-permute-start.14
  140.9 1.1 collective-permute-done.13.refs_1_
  142.6 1.5 collective-permute-done.15.refs_3_
  144.1 3.5 %shard_map.62 = (f32[1,4096]{1,0:T(1,128)S(1)}, f32[1,4096]{1,0:T(1,128)S(1)}, f32[1,1024]{1,0:T(1,128)S(1)}, f32[1,4096]{1,0:T(1,128)S(1)}) custom-call(f32[1,4096]{1,0:T(1,128)S(1)} %add.31.refs_0_, f32[1,4096]{1,0:T(1,128)S(1)} %collective-permute-done.13.refs_1_, f32[1,4096]{1,0:T(1,128)S(1)} %collective-permute-done.14.refs_2_, ...), custom_call_target="tpu_custom_call" | custom-call | tf_op jit(solution)/shard_map/pallas_call | solution.py:341
  147.7 1.2 collective-permute-done.18
  148.9 0.8 collective-permute-start.19
  149.7 1.3 collective-permute-start.20
  151.0 1.5 collective-permute-start.21
  152.5 1.1 collective-permute-done.19.refs_1_
  153.6 1.1 collective-permute-done.21.refs_3_
  154.7 3.5 %shard_map.63 = (f32[1,4096]{1,0:T(1,128)S(1)}, f32[1,4096]{1,0:T(1,128)S(1)}, f32[1,4096]{1,0:T(1,128)S(1)}, f32[1,1024]{1,0:T(1,128)S(1)}, f32[1,1024]{1,0:T(1,128)S(1)}, /*index=5*/f32[1,4096]{1,0:T(1,128)S(1)}) custom-call(f32[1,4096]{1,0:T(1,128)S(1)} %add.33.refs_0_, f32[1,4096]{1,0:T(1,128)S(1)} %collective-permute-done.19.refs_1_, ...), custom_call_target="tpu_custom_call" | custom-call | tf_op jit(solution)/shard_map/pallas_call | solution.py:341
  158.3 1.2 collective-permute-done.22
  159.5 1.5 collective-permute-start.23
  161.0 1.5 collective-permute-start.24
  163.0 1.1 collective-permute-done.23.refs_1_
  164.8 1.5 collective-permute-done.25.refs_3_
  166.3 3.7 %shard_map.64 = (f32[1,4096]{1,0:T(1,128)S(1)}, f32[1,4096]{1,0:T(1,128)S(1)}, f32[1,4096]{1,0:T(1,128)S(1)}, f32[1,1024]{1,0:T(1,128)S(1)}, f32[1,1024]{1,0:T(1,128)S(1)}, /*index=5*/f32[1,4096]{1,0:T(1,128)S(1)}) custom-call(f32[1,4096]{1,0:T(1,128)S(1)} %add.34.refs_0_, f32[1,4096]{1,0:T(1,128)S(1)} %collective-permute-done.23.refs_1_, ...), custom_call_target="tpu_custom_call" | custom-call | tf_op jit(solution)/shard_map/pallas_call | solution.py:341
  170.1 1.2 collective-permute-done.26
  171.3 0.8 collective-permute-start.27
  172.0 1.3 collective-permute-start.28
  173.3 1.5 collective-permute-start.29
  174.8 1.1 collective-permute-done.27.refs_1_
  176.0 1.1 collective-permute-done.29.refs_3_
  177.0 6.4 %shard_map.65 = (f32[64,256]{1,0:T(8,128)S(1)}, f32[64,256]{1,0:T(8,128)S(1)}, f32[8,136,128]{2,1,0:T(8,128)S(1)}, f32[8,128]{1,0:T(8,128)S(1)}) custom-call(f32[1,4096]{1,0:T(1,128)S(1)} %add.35.refs_0_, f32[1,4096]{1,0:T(1,128)S(1)} %collective-permute-done.27.refs_1_, f32[1,4096]{1,0:T(1,128)S(1)} %collective-permute-done.28.refs_2_, ...), custom_call_target="tpu_custom_call" | custom-call | tf_op jit(solution)/shard_map/pallas_call | solution.py:341
  183.5 1.5 collective-permute-done.30
  185.1 1.5 collective-permute-start.31
  186.7 1.5 collective-permute-start.32
  188.7 2.5 %collective-permute-done.31.refs_1_ = f32[1,136,128]{2,1,0:T(8,128)S(1)} collective-permute-done((f32[1,136,128]{2,1,0:T(8,128)S(1)}, f32[1,136,128]{2,1,0:T(8,128)S(1)}, u32[]{:S(2)}, u32[]{:S(2)}) %collective-permute-start.31) | collective-permute-done | bytes 69664 | tf_op jit(solution)/shard_map/ppermute | solution.py:368
  (61 shorter events, 8.5 us)
Async XLA Ops:
  0.6 135.5 %copy-start.3 = (f32[1024]{0:T(1024)S(1)}, f32[1024]{0:T(1024)}, u32[]{:S(2)}) copy-start(f32[1024]{0:T(1024)} %param.7) | copy-start | bytes 12292
  0.6 20.5 %collective-permute-start = (bf16[1,64,256]{2,1,0:T(8,128)(2,1)}, bf16[1,64,256]{2,1,0:T(8,128)(2,1)S(1)}, u32[]{:S(2)}, u32[]{:S(2)}) collective-permute-start(bf16[1,64,256]{2,1,0:T(8,128)(2,1)} %bitcast.38), channel_id=1, source_target_pairs={{0,8},{1,9},{2,10},{3,11},{4,12},{5,13},{6,14},{7,15},{8,0},{9,1},... | collective-permute-start | bytes 98312 | tf_op jit(solution)/shard_map/ppermute | solution.py:368
  3.8 3.9 %collective-permute-start.2 = (bf16[1,64,128]{2,1,0:T(8,128)(2,1)}, bf16[1,64,128]{2,1,0:T(8,128)(2,1)S(1)}, u32[]{:S(2)}, u32[]{:S(2)}) collective-permute-start(bf16[1,64,128]{2,1,0:T(8,128)(2,1)} %bitcast.39), channel_id=1, source_target_pairs={{0,8},{1,9},{2,10},{3,11},{4,12},{5,13},{6,14},{7,15},{8,0},{9,1},... | collective-permute-start | bytes 49160 | tf_op jit(solution)/shard_map/ppermute | solution.py:368
  3.8 0.8 copy-start
  4.6 0.7 copy-start.1
  5.3 0.7 copy-start.2
  7.7 5.0 %collective-permute-start.3 = (bf16[2,64,128]{2,1,0:T(8,128)(2,1)S(1)}, bf16[2,64,128]{2,1,0:T(8,128)(2,1)S(1)}, u32[]{:S(2)}, u32[]{:S(2)}) collective-permute-start(bf16[2,64,128]{2,1,0:T(8,128)(2,1)S(1)} %pad_maximum_fusion.1), channel_id=1, source_target_pairs={{0,16},{1,17},{2,18},{3,19},{4,20},{5,21},{6,22},{7,23},{8,24},{9,... | collective-permute-start | bytes 98312 | tf_op jit(solution)/shard_map/ppermute | solution.py:368
  12.7 5.0 %collective-permute-start.4 = (bf16[4,64,128]{2,1,0:T(8,128)(2,1)S(1)}, bf16[4,64,128]{2,1,0:T(8,128)(2,1)S(1)}, u32[]{:S(2)}, u32[]{:S(2)}) collective-permute-start(bf16[4,64,128]{2,1,0:T(8,128)(2,1)S(1)} %get-tuple-element.84), channel_id=1, source_target_pairs={{0,2},{1,3},{2,0},{3,1},{4,6},{5,7},{6,4},{7,5},{8,10},{9,11},{10,... | collective-permute-start | bytes 196616 | tf_op jit(solution)/shard_map/ppermute | solution.py:368
  14.4 4.3 %collective-permute-start.5 = (bf16[4,64,128]{2,1,0:T(8,128)(2,1)S(1)}, bf16[4,64,128]{2,1,0:T(8,128)(2,1)S(1)}, u32[]{:S(2)}, u32[]{:S(2)}) collective-permute-start(bf16[4,64,128]{2,1,0:T(8,128)(2,1)S(1)} %get-tuple-element.84), channel_id=1, source_target_pairs={{0,4},{1,5},{2,6},{3,7},{4,0},{5,1},{6,2},{7,3},{8,12},{9,13},{10,... | collective-permute-start | bytes 196616 | tf_op jit(solution)/shard_map/ppermute | solution.py:368
  15.9 5.2 %collective-permute-start.6 = (bf16[4,64,128]{2,1,0:T(8,128)(2,1)S(1)}, bf16[4,64,128]{2,1,0:T(8,128)(2,1)S(1)}, u32[]{:S(2)}, u32[]{:S(2)}) collective-permute-start(bf16[4,64,128]{2,1,0:T(8,128)(2,1)S(1)} %get-tuple-element.84), channel_id=1, source_target_pairs={{0,6},{1,7},{2,4},{3,5},{4,2},{5,3},{6,0},{7,1},{8,14},{9,15},{10,... | collective-permute-start | bytes 196616 | tf_op jit(solution)/shard_map/ppermute | solution.py:368
  21.1 6.6 %collective-permute-start.7 = (bf16[16,64,128]{2,1,0:T(8,128)(2,1)S(1)}, bf16[16,64,128]{2,1,0:T(8,128)(2,1)S(1)}, u32[]{:S(2)}, u32[]{:S(2)}) collective-permute-start(bf16[16,64,128]{2,1,0:T(8,128)(2,1)S(1)} %get-tuple-element.76), channel_id=1, source_target_pairs={{0,1},{1,0},{2,3},{3,2},{4,5},{5,4},{6,7},{7,6},{8,9},{9,8},{10,11... | collective-permute-start | bytes 786440 | tf_op jit(solution)/shard_map/ppermute | solution.py:368
  21.2 6.5 %collective-permute-start.1 = (bf16[2,64,256]{2,1,0:T(8,128)(2,1)S(1)}, bf16[2,64,256]{2,1,0:T(8,128)(2,1)S(1)}, u32[]{:S(2)}, u32[]{:S(2)}) collective-permute-start(bf16[2,64,256]{2,1,0:T(8,128)(2,1)S(1)} %pad_maximum_fusion), channel_id=1, source_target_pairs={{0,16},{1,17},{2,18},{3,19},{4,20},{5,21},{6,22},{7,23},{8,24},{9,... | collective-permute-start | bytes 196616 | tf_op jit(solution)/shard_map/ppermute | solution.py:368
  82.1 1.2 collective-permute-start.8
  82.3 4.7 %collective-permute-start.16 = (f32[1,256]{1,0:T(1,128)S(1)}, f32[1,256]{1,0:T(1,128)S(1)}, u32[]{:S(2)}, u32[]{:S(2)}) collective-permute-start(f32[1,256]{1,0:T(1,128)S(1)} %get-tuple-element.49), channel_id=1, source_target_pairs={{0,8},{1,9},{2,10},{3,11},{4,12},{5,13},{6,14},{7,15},{8,0},{9,1},... | collective-permute-start | bytes 3080 | tf_op jit(solution)/shard_map/ppermute | solution.py:368
  83.4 5.7 %collective-permute-start.9 = (f32[1,4096]{1,0:T(1,128)S(1)}, f32[1,4096]{1,0:T(1,128)S(1)}, u32[]{:S(2)}, u32[]{:S(2)}) collective-permute-start(f32[1,4096]{1,0:T(1,128)S(1)} %multiply_add_fusion.refs_0_), channel_id=1, source_target_pairs={{0,6},{1,7},{2,4},{3,5},{4,2},{5,3},{6,0},{7,1},{8,14},{9,15},{10,... | collective-permute-start | bytes 49160 | tf_op jit(solution)/shard_map/ppermute | solution.py:368
  84.2 4.9 %collective-permute-start.10 = (f32[1,4096]{1,0:T(1,128)S(1)}, f32[1,4096]{1,0:T(1,128)S(1)}, u32[]{:S(2)}, u32[]{:S(2)}) collective-permute-start(f32[1,4096]{1,0:T(1,128)S(1)} %multiply_add_fusion.refs_0_), channel_id=1, source_target_pairs={{0,4},{1,5},{2,6},{3,7},{4,0},{5,1},{6,2},{7,3},{8,12},{9,13},{10,... | collective-permute-start | bytes 49160 | tf_op jit(solution)/shard_map/ppermute | solution.py:368
  85.5 3.7 %collective-permute-start.11 = (f32[1,4096]{1,0:T(1,128)S(1)}, f32[1,4096]{1,0:T(1,128)S(1)}, u32[]{:S(2)}, u32[]{:S(2)}) collective-permute-start(f32[1,4096]{1,0:T(1,128)S(1)} %multiply_add_fusion.refs_0_), channel_id=1, source_target_pairs={{0,2},{1,3},{2,0},{3,1},{4,6},{5,7},{6,4},{7,5},{8,10},{9,11},{10,... | collective-permute-start | bytes 49160 | tf_op jit(solution)/shard_map/ppermute | solution.py:368
  87.0 53.9 %collective-permute-start.17 = (f32[2,256]{1,0:T(2,128)S(1)}, f32[2,256]{1,0:T(2,128)S(1)}, u32[]{:S(2)}, u32[]{:S(2)}) collective-permute-start(f32[2,256]{1,0:T(2,128)S(1)} %pad_maximum_fusion.2), channel_id=1, source_target_pairs={{0,16},{1,17},{2,18},{3,19},{4,20},{5,21},{6,22},{7,23},{8,24},{9,... | collective-permute-start | bytes 6152 | tf_op jit(solution)/shard_map/ppermute | solution.py:368
  136.1 1.2 collective-permute-start.12
  137.4 4.7 %collective-permute-start.13 = (f32[1,4096]{1,0:T(1,128)S(1)}, f32[1,4096]{1,0:T(1,128)S(1)}, u32[]{:S(2)}, u32[]{:S(2)}) collective-permute-start(f32[1,4096]{1,0:T(1,128)S(1)} %add.31.refs_0_), channel_id=1, source_target_pairs={{0,6},{1,7},{2,4},{3,5},{4,2},{5,3},{6,0},{7,1},{8,14},{9,15},{10,... | collective-permute-start | bytes 49160 | tf_op jit(solution)/shard_map/ppermute | solution.py:368
  138.9 3.7 %collective-permute-start.14 = (f32[1,4096]{1,0:T(1,128)S(1)}, f32[1,4096]{1,0:T(1,128)S(1)}, u32[]{:S(2)}, u32[]{:S(2)}) collective-permute-start(f32[1,4096]{1,0:T(1,128)S(1)} %add.31.refs_0_), channel_id=1, source_target_pairs={{0,4},{1,5},{2,6},{3,7},{4,0},{5,1},{6,2},{7,3},{8,12},{9,13},{10,... | collective-permute-start | bytes 49160 | tf_op jit(solution)/shard_map/ppermute | solution.py:368
  140.4 3.7 %collective-permute-start.15 = (f32[1,4096]{1,0:T(1,128)S(1)}, f32[1,4096]{1,0:T(1,128)S(1)}, u32[]{:S(2)}, u32[]{:S(2)}) collective-permute-start(f32[1,4096]{1,0:T(1,128)S(1)} %add.31.refs_0_), channel_id=1, source_target_pairs={{0,2},{1,3},{2,0},{3,1},{4,6},{5,7},{6,4},{7,5},{8,10},{9,11},{10,... | collective-permute-start | bytes 49160 | tf_op jit(solution)/shard_map/ppermute | solution.py:368
  147.7 1.2 collective-permute-start.18
  148.9 4.7 %collective-permute-start.19 = (f32[1,4096]{1,0:T(1,128)S(1)}, f32[1,4096]{1,0:T(1,128)S(1)}, u32[]{:S(2)}, u32[]{:S(2)}) collective-permute-start(f32[1,4096]{1,0:T(1,128)S(1)} %add.33.refs_0_), channel_id=1, source_target_pairs={{0,6},{1,7},{2,4},{3,5},{4,2},{5,3},{6,0},{7,1},{8,14},{9,15},{10,... | collective-permute-start | bytes 49160 | tf_op jit(solution)/shard_map/ppermute | solution.py:368
  149.7 3.9 %collective-permute-start.20 = (f32[1,4096]{1,0:T(1,128)S(1)}, f32[1,4096]{1,0:T(1,128)S(1)}, u32[]{:S(2)}, u32[]{:S(2)}) collective-permute-start(f32[1,4096]{1,0:T(1,128)S(1)} %add.33.refs_0_), channel_id=1, source_target_pairs={{0,4},{1,5},{2,6},{3,7},{4,0},{5,1},{6,2},{7,3},{8,12},{9,13},{10,... | collective-permute-start | bytes 49160 | tf_op jit(solution)/shard_map/ppermute | solution.py:368
  151.0 3.7 %collective-permute-start.21 = (f32[1,4096]{1,0:T(1,128)S(1)}, f32[1,4096]{1,0:T(1,128)S(1)}, u32[]{:S(2)}, u32[]{:S(2)}) collective-permute-start(f32[1,4096]{1,0:T(1,128)S(1)} %add.33.refs_0_), channel_id=1, source_target_pairs={{0,2},{1,3},{2,0},{3,1},{4,6},{5,7},{6,4},{7,5},{8,10},{9,11},{10,... | collective-permute-start | bytes 49160 | tf_op jit(solution)/shard_map/ppermute | solution.py:368
  158.2 1.2 collective-permute-start.22
  159.5 4.7 %collective-permute-start.23 = (f32[1,4096]{1,0:T(1,128)S(1)}, f32[1,4096]{1,0:T(1,128)S(1)}, u32[]{:S(2)}, u32[]{:S(2)}) collective-permute-start(f32[1,4096]{1,0:T(1,128)S(1)} %add.34.refs_0_), channel_id=1, source_target_pairs={{0,6},{1,7},{2,4},{3,5},{4,2},{5,3},{6,0},{7,1},{8,14},{9,15},{10,... | collective-permute-start | bytes 49160 | tf_op jit(solution)/shard_map/ppermute | solution.py:368
  161.0 3.7 %collective-permute-start.24 = (f32[1,4096]{1,0:T(1,128)S(1)}, f32[1,4096]{1,0:T(1,128)S(1)}, u32[]{:S(2)}, u32[]{:S(2)}) collective-permute-start(f32[1,4096]{1,0:T(1,128)S(1)} %add.34.refs_0_), channel_id=1, source_target_pairs={{0,4},{1,5},{2,6},{3,7},{4,0},{5,1},{6,2},{7,3},{8,12},{9,13},{10,... | collective-permute-start | bytes 49160 | tf_op jit(solution)/shard_map/ppermute | solution.py:368
  162.5 3.7 %collective-permute-start.25 = (f32[1,4096]{1,0:T(1,128)S(1)}, f32[1,4096]{1,0:T(1,128)S(1)}, u32[]{:S(2)}, u32[]{:S(2)}) collective-permute-start(f32[1,4096]{1,0:T(1,128)S(1)} %add.34.refs_0_), channel_id=1, source_target_pairs={{0,2},{1,3},{2,0},{3,1},{4,6},{5,7},{6,4},{7,5},{8,10},{9,11},{10,... | collective-permute-start | bytes 49160 | tf_op jit(solution)/shard_map/ppermute | solution.py:368
  170.0 1.2 collective-permute-start.26
  171.3 4.7 %collective-permute-start.27 = (f32[1,4096]{1,0:T(1,128)S(1)}, f32[1,4096]{1,0:T(1,128)S(1)}, u32[]{:S(2)}, u32[]{:S(2)}) collective-permute-start(f32[1,4096]{1,0:T(1,128)S(1)} %add.35.refs_0_), channel_id=1, source_target_pairs={{0,6},{1,7},{2,4},{3,5},{4,2},{5,3},{6,0},{7,1},{8,14},{9,15},{10,... | collective-permute-start | bytes 49160 | tf_op jit(solution)/shard_map/ppermute | solution.py:368
  172.0 3.9 %collective-permute-start.28 = (f32[1,4096]{1,0:T(1,128)S(1)}, f32[1,4096]{1,0:T(1,128)S(1)}, u32[]{:S(2)}, u32[]{:S(2)}) collective-permute-start(f32[1,4096]{1,0:T(1,128)S(1)} %add.35.refs_0_), channel_id=1, source_target_pairs={{0,4},{1,5},{2,6},{3,7},{4,0},{5,1},{6,2},{7,3},{8,12},{9,13},{10,... | collective-permute-start | bytes 49160 | tf_op jit(solution)/shard_map/ppermute | solution.py:368
  173.3 3.7 %collective-permute-start.29 = (f32[1,4096]{1,0:T(1,128)S(1)}, f32[1,4096]{1,0:T(1,128)S(1)}, u32[]{:S(2)}, u32[]{:S(2)}) collective-permute-start(f32[1,4096]{1,0:T(1,128)S(1)} %add.35.refs_0_), channel_id=1, source_target_pairs={{0,2},{1,3},{2,0},{3,1},{4,6},{5,7},{6,4},{7,5},{8,10},{9,11},{10,... | collective-permute-start | bytes 49160 | tf_op jit(solution)/shard_map/ppermute | solution.py:368
  183.4 1.6 collective-permute-start.30
  185.1 6.0 %collective-permute-start.31 = (f32[1,136,128]{2,1,0:T(8,128)S(1)}, f32[1,136,128]{2,1,0:T(8,128)S(1)}, u32[]{:S(2)}, u32[]{:S(2)}) collective-permute-start(f32[1,136,128]{2,1,0:T(8,128)S(1)} %get-tuple-element.74), channel_id=1, source_target_pairs={{0,6},{1,7},{2,4},{3,5},{4,2},{5,3},{6,0},{7,1},{8,14},{9,15},{10,... | collective-permute-start | bytes 208904 | tf_op jit(solution)/shard_map/ppermute | solution.py:368
  186.7 5.2 %collective-permute-start.32 = (f32[1,136,128]{2,1,0:T(8,128)S(1)}, f32[1,136,128]{2,1,0:T(8,128)S(1)}, u32[]{:S(2)}, u32[]{:S(2)}) collective-permute-start(f32[1,136,128]{2,1,0:T(8,128)S(1)} %get-tuple-element.73), channel_id=1, source_target_pairs={{0,4},{1,5},{2,6},{3,7},{4,0},{5,1},{6,2},{7,3},{8,12},{9,13},{10,... | collective-permute-start | bytes 208904 | tf_op jit(solution)/shard_map/ppermute | solution.py:368
  188.2 4.3 %collective-permute-start.33 = (f32[1,136,128]{2,1,0:T(8,128)S(1)}, f32[1,136,128]{2,1,0:T(8,128)S(1)}, u32[]{:S(2)}, u32[]{:S(2)}) collective-permute-start(f32[1,136,128]{2,1,0:T(8,128)S(1)} %get-tuple-element.72), channel_id=1, source_target_pairs={{0,2},{1,3},{2,0},{3,1},{4,6},{5,7},{6,4},{7,5},{8,10},{9,11},{10,... | collective-permute-start | bytes 208904 | tf_op jit(solution)/shard_map/ppermute | solution.py:368
